TPU v7x, 256 devices: a whole 4x4x8 slice. The times are simulated.
256 devices in a mesh: tile: 32 (over y_hi, z, core), slide: 8 (over x, y_lo).
Axes of the slice: x: 4, y: 4 (y_hi: 2, y_lo: 2; y = y_hi * 2 + y_lo), z: 8, core: 2. Of those that a mesh axis runs over, the one named last changes fastest.
Arguments:
- tokens: bfloat16 [768, 64, 384], P(('slide', 'tile')), parts along dimension 0, may hold values from -6 to 6
- tissue: int32 [768, 64], P(('slide', 'tile')), parts along dimension 0, may hold values from 0 to 1, as said below
- dw_kernel: bfloat16 [7, 7, 384], replicated, may hold values from -0.875 to 0.875
- w_fc1: bfloat16 [384, 1536], replicated, may hold values from -0.3125 to 0.3125
- w_fc2: bfloat16 [1536, 384], replicated, may hold values from -0.15625 to 0.15625
- layer_scale: float32 [384], replicated, may hold values from 0.3 to 3
- w_query: bfloat16 [384, 1024], replicated, may hold values from -16 to 16
- w_key: bfloat16 [384, 1024], replicated, may hold values from -0.3125 to 0.3125
- w_value: bfloat16 [384, 1024], replicated, may hold values from -0.3125 to 0.3125
- w_out: bfloat16 [1024, 384], replicated, may hold values from -0.1875 to 0.1875
Outputs:
- encoded: bfloat16 [768, 64, 384], P(('slide', 'tile')), parts along dimension 0
There are 8 independent parts, one for each index of `slide`. A program takes and returns all parts, laid end to end along the dimension named above; an argument that names none is the same for every part. Nothing has to cross between parts.
Inputs may be any that keep to these rules, and one draw needn't show every extreme that they name: Among the 192 tiles of each aligned block of 3 grid rows at most 96 hold tissue, and at least one; some block holds exactly 96.
All inputs are finite; a program needn't handle non-finite values.
Results may differ from a plain program's by a relative error of at most 0.035.
Values may be sent and summed in bfloat16 or wider, within the bound.
A program may use at most 192 MiB of HBM per device.

v0:
```python
import jax
import jax.numpy as jnp
from jax import lax
from jax.sharding import PartitionSpec as P

HEADS = 16
HD = 64
CAP = 96


def padded_2(block, sides, width):
    for axis, dim in sides:
        count = lax.axis_size(axis)
        forward = [(i, i + 1) for i in range(count - 1)]
        backward = [(target, source) for source, target in forward]
        low = lax.ppermute(
            lax.slice_in_dim(block, block.shape[dim] - width, None, axis=dim), axis, forward
        )
        high = lax.ppermute(lax.slice_in_dim(block, 0, width, axis=dim), axis, backward)
        block = jnp.concatenate([low, block, high], axis=dim)
    return block


def from_everyone(x, axis):
    copies = jnp.broadcast_to(x, (lax.axis_size(axis), *x.shape))
    return lax.all_to_all(copies, axis, split_axis=0, concat_axis=0, tiled=True)


def in_order(tiles, dim):
    tiles = jnp.moveaxis(tiles, 0, dim)
    shape = tiles.shape
    return tiles.reshape(*shape[:dim], shape[dim] * shape[dim + 1], *shape[dim + 2 :])


def collect(x, axis, dim):
    tiles = from_everyone(x, axis)
    return in_order(tiles, dim)


def layer_norm(x):
    mean = jnp.mean(x, axis=-1, keepdims=True)
    centred = x - mean
    var = jnp.mean(centred * centred, axis=-1, keepdims=True)
    return centred * lax.rsqrt(var + 1e-06)


def attend(carry, query_heads, keys, values, flags):
    count = keys.shape[0]
    key_heads = jnp.transpose(keys.reshape(count, HEADS, HD), (1, 0, 2))
    value_heads = jnp.transpose(values.reshape(count, HEADS, HD), (1, 0, 2))
    live = flags > 0

    def one_head(inputs):
        q_head, k_head, v_head, run_max, run_sum, run_acc = inputs
        scores = jnp.einsum("qd,kd->qk", q_head, k_head, preferred_element_type=jnp.float32) * 0.125
        scores = jnp.where(live[None, :], scores, -1e30)
        new_max = jnp.maximum(run_max, jnp.max(scores, axis=1))
        factor = jnp.exp(run_max - new_max)
        weights = jnp.where(live[None, :], jnp.exp(scores - new_max[:, None]), 0.0)
        new_sum = run_sum * factor + jnp.sum(weights, axis=1)
        new_acc = run_acc * factor[:, None] + jnp.dot(
            weights.astype(jnp.bfloat16), v_head, preferred_element_type=jnp.float32
        )
        return (new_max, new_sum, new_acc)

    run_max, run_sum, run_acc = carry
    return lax.map(one_head, (query_heads, key_heads, value_heads, run_max, run_sum, run_acc))


def local(tokens, tissue, dw_kernel, w_fc1, w_fc2, layer_scale, w_query, w_key, w_value, w_out):
    rows_dev, width, chans = tokens.shape
    masked = tokens * tissue[:, :, None].astype(jnp.bfloat16)
    extended = padded_2(masked, (("tile", 0),), 3)
    padded = jnp.pad(extended, ((0, 0), (3, 3), (0, 0))).astype(jnp.float32)
    kernel = dw_kernel.astype(jnp.float32)
    conv = jnp.zeros((rows_dev, width, chans), jnp.float32)
    for offs_i in range(7):
        for offs_j in range(7):
            conv = (
                conv
                + padded[offs_i : offs_i + rows_dev, offs_j : offs_j + width]
                * kernel[offs_i, offs_j]
            )
    ntok = rows_dev * width
    flat_masked = masked.reshape(ntok, chans)
    normed1 = layer_norm(conv.reshape(ntok, chans)).astype(jnp.bfloat16)
    hidden = jax.nn.gelu(
        jnp.dot(normed1, w_fc1, preferred_element_type=jnp.float32), approximate=False
    ).astype(jnp.bfloat16)
    branch = jnp.dot(hidden, w_fc2, preferred_element_type=jnp.float32)
    section = (flat_masked.astype(jnp.float32) + layer_scale * branch).astype(jnp.bfloat16)
    normed2 = layer_norm(section.astype(jnp.float32)).astype(jnp.bfloat16)
    query = jnp.dot(normed2, w_query, preferred_element_type=jnp.float32).astype(jnp.bfloat16)
    query_heads = jnp.transpose(query.reshape(ntok, HEADS, HD), (1, 0, 2))
    flags = tissue.reshape(ntok)
    start_state = (
        jnp.full((HEADS, ntok), -1e30, jnp.float32),
        jnp.zeros((HEADS, ntok), jnp.float32),
        jnp.zeros((HEADS, ntok, HD), jnp.float32),
    )
    order = jnp.argsort(1 - flags, stable=True)[:CAP]
    rows_in = collect(normed2[order], "tile", 0)
    flags_in = collect(flags[order], "tile", 0)
    keys = jnp.dot(rows_in, w_key, preferred_element_type=jnp.float32).astype(jnp.bfloat16)
    values = jnp.dot(rows_in, w_value, preferred_element_type=jnp.float32).astype(jnp.bfloat16)
    run_max, run_sum, run_acc = attend(start_state, query_heads, keys, values, flags_in)
    attended = (run_acc / run_sum[:, :, None]).astype(jnp.bfloat16)
    attended = jnp.transpose(attended, (1, 0, 2)).reshape(ntok, HEADS * HD)
    result = section.astype(jnp.float32) + jnp.dot(
        attended, w_out, preferred_element_type=jnp.float32
    )
    return result.astype(jnp.bfloat16).reshape(rows_dev, width, chans)


def solution(mesh):
    in_specs = (
        P(("slide", "tile"), None, None),
        P(("slide", "tile"), None),
        P(),
        P(),
        P(),
        P(),
        P(),
        P(),
        P(),
        P(),
    )
    out_specs = P(("slide", "tile"), None, None)
    return jax.shard_map(local, mesh=mesh, in_specs=in_specs, out_specs=out_specs, check_vma=False)
```

profile of v0, /device:TPU:1, one launch (start us, length us, event | category | flops | bytes accessed | tf_op | source)
XLA Modules:
  0.0 212.5 jit_solution(17334434237015063328)
XLA Ops:
  1.8 4.9 %collective-permute-start = (bf16[3,64,384]{2,1,0:T(8,128)(2,1)S(1)}, bf16[3,64,384]{2,1,0:T(8,128)(2,1)S(1)}, u32[]{:S(2)}, u32[]{:S(2)}) collective-permute-start(bf16[3,64,384]{2,1,0:T(8,128)(2,1)S(1)} %broadcast_multiply_fusion), channel_id=1, source_target_pairs={{0,8},{8,16},{16,24},{24,32},{32,40},{40,48},{48,56},{56,64},{64,7... | collective-permute-start | bytes 442376 | tf_op jit(solution)/shard_map/ppermute | solution.py:16
  6.7 1.9 collective-permute-start.1
  9.4 3.2 %sort.17 = (s32[192]{0:T(256)}, s32[192]{0:T(256)S(1)}) sort(s32[192]{0:T(256)S(1)} %broadcast_subtract_fusion, s32[192]{0:T(256)S(1)} %iota.4), dimensions={0}, to_apply=%region_4.5 | sort | flops 1536 | bytes 3072 | tf_op jit(solution)/shard_map/jit(argsort)/sort | solution.py:101
  14.5 12.7 %all-to-all-start = ((s32[32,1,96]{2,1,0:T(1,128)}), s32[32,1,96]{2,1,0:T(1,128)S(1)}, u32[]{:S(2)}, u32[]{:S(2)}) async-start(s32[32,1,96]{2,1,0:T(1,128)} %broadcast_in_dim.47), calls=%async_computation | async-start | bytes 32768 | tf_op jit(solution)/shard_map/all_to_all | solution.py:26
  28.4 2.2 %fusion.158 = (f32[3,64]{1,0:T(4,128)S(1)}, f32[3,64,384]{2,1,0:T(8,128)S(1)}) fusion(f32[384]{0:T(512)S(1)} %get-tuple-element.62, f32[9,70,384]{2,1,0:T(8,128)S(1)} %fusion.77, f32[384]{0:T(512)S(1)} %get-tuple-element.63, f32[384]{0:T(512)S(1)} %get-tuple-element.64, f32[384]{0:T(512)S(1)} %get-tuple-element.65, f32[384]{0:T(512)S(1)} %get-tuple-element.66, ...), kind=kLoop, calls=%fused_computation.284 | loop fusion | flops 7225152 | bytes 14821632 | tf_op jit(solution)/shard_map/reduce_sum | solution.py:41
  31.1 3.2 %fusion.161 = (f32[192]{0:T(256)S(1)}, f32[192,384]{1,0:T(8,128)S(1)}) fusion(bf16[1536,384]{1,0:T(8,128)(2,1)S(1)} %copy-done, f32[384]{0:T(512)S(1)} %copy-done.3, bf16[192,384]{1,0:T(8,128)(2,1)S(1)} %bitcast.66, bf16[192,384]{1,0:T(8,128)(2,1)S(1)} %fusion.127, bf16[384,1536]{1,0:T(8,128)(2,1)S(1)} %copy-done.2), kind=kOutput, calls=%fused_computation.286 | convolution fusion | flops 472596288 | bytes 2951424 | tf_op jit(solution)/shard_map/dot_general | solution.py:90
  38.1 8.9 %all-to-all-start.1 = ((bf16[32,96,384]{2,1,0:T(8,128)(2,1)}), bf16[32,96,384]{2,1,0:T(8,128)(2,1)}, u32[]{:S(2)}, u32[]{:S(2)}) async-start(bf16[32,96,384]{2,1,0:T(8,128)(2,1)} %broadcast_in_dim.48), calls=%async_computation.1 | async-start | bytes 4718592 | tf_op jit(solution)/shard_map/all_to_all | solution.py:26
  49.7 53.9 %all-to-all-done.1 = bf16[32,96,384]{2,1,0:T(8,128)(2,1)} async-done(((bf16[32,96,384]{2,1,0:T(8,128)(2,1)}), bf16[32,96,384]{2,1,0:T(8,128)(2,1)}, u32[]{:S(2)}, u32[]{:S(2)}) %all-to-all-start.1) | async-done | bytes 2359328 | tf_op jit(solution)/shard_map/all_to_all | solution.py:26
  103.7 7.9 %convolution_convert_fusion.1 = bf16[3072,1024]{0,1:T(8,128)(2,1)} fusion(bf16[3072,384]{1,0:T(8,128)(2,1)} %bitcast.9, bf16[384,1024]{1,0:T(8,128)(2,1)} %param.19), kind=kOutput, calls=%fused_computation.27 | convolution fusion | flops 2419064832 | bytes 9437184 | tf_op jit(solution)/shard_map/dot_general | solution.py:104
  111.6 12.0 %copy.19 = bf16[3072,16,64]{2,0,1:T(8,128)(2,1)} copy(bf16[3072,16,64]{0,2,1:T(8,128)(2,1)} %bitcast.63) | data formatting | bytes 12582912 | tf_op jit(solution)/shard_map/reshape | solution.py:49
  123.6 8.0 %convolution_convert_fusion = bf16[3072,1024]{0,1:T(8,128)(2,1)} fusion(bf16[3072,384]{1,0:T(8,128)(2,1)} %bitcast.9, bf16[384,1024]{1,0:T(8,128)(2,1)} %param.20), kind=kOutput, calls=%fused_computation.26 | convolution fusion | flops 2419064832 | bytes 9437184 | tf_op jit(solution)/shard_map/dot_general | solution.py:105
  131.7 12.1 %copy.20 = bf16[3072,16,64]{2,0,1:T(8,128)(2,1)} copy(bf16[3072,16,64]{0,2,1:T(8,128)(2,1)} %bitcast.62) | data formatting | bytes 12582912 | tf_op jit(solution)/shard_map/reshape | solution.py:50
  143.7 66.6 %while.12 = (s32[]{:T(128)}, f32[16,192]{1,0:T(8,128)S(1)}, f32[16,192,64]{1,2,0:T(8,128)S(1)}, pred[3072]{0:T(1024)(128)(4,1)S(1)}, bf16[16,192,64]{1,2,0:T(8,1...) while((s32[]{:T(128)}, f32[16,192]{1,0:T(8,128)S(1)}, ...), condition=%wide.region_8.9_spmd, body=%wide.region_5.8_spmd.sunk | while | flops 156316224 | bytes 8770913 | solution.py:67
  143.7 1.7 fusion.182
  146.0 1.7 fusion.184
  147.9 1.8 fusion.182
  152.0 1.8 fusion.182
  154.4 1.7 fusion.184
  156.2 1.8 fusion.182
  160.4 1.8 fusion.182
  162.7 1.7 fusion.184
  164.5 1.8 fusion.182
  168.7 1.8 fusion.182
  172.9 1.8 fusion.182
  177.0 1.8 fusion.182
  181.2 1.8 fusion.182
  185.3 1.8 fusion.182
  189.5 1.8 fusion.182
  193.7 1.8 fusion.182
  197.8 1.8 fusion.182
  202.0 1.8 fusion.182
  206.2 1.8 fusion.182
  (122 shorter events, 47.4 us)
Async XLA Ops:
  0.0 31.1 %copy-start = (bf16[1536,384]{1,0:T(8,128)(2,1)S(1)}, bf16[1536,384]{1,0:T(8,128)(2,1)}, u32[]{:S(2)}) copy-start(bf16[1536,384]{1,0:T(8,128)(2,1)} %param.16) | copy-start | bytes 3538948
  1.8 26.4 %collective-permute-start = (bf16[3,64,384]{2,1,0:T(8,128)(2,1)S(1)}, bf16[3,64,384]{2,1,0:T(8,128)(2,1)S(1)}, u32[]{:S(2)}, u32[]{:S(2)}) collective-permute-start(bf16[3,64,384]{2,1,0:T(8,128)(2,1)S(1)} %broadcast_multiply_fusion), channel_id=1, source_target_pairs={{0,8},{8,16},{16,24},{24,32},{32,40},{40,48},{48,56},{56,64},{64,7... | collective-permute-start | bytes 442376 | tf_op jit(solution)/shard_map/ppermute | solution.py:16
  6.7 21.5 %collective-permute-start.1 = (bf16[3,64,384]{2,1,0:T(8,128)(2,1)S(1)}, bf16[3,64,384]{2,1,0:T(8,128)(2,1)S(1)}, u32[]{:S(2)}, u32[]{:S(2)}) collective-permute-start(bf16[3,64,384]{2,1,0:T(8,128)(2,1)S(1)} %broadcast_multiply_fusion), channel_id=1, source_target_pairs={{8,0},{16,8},{24,16},{32,24},{40,32},{48,40},{56,48},{64,56},{72,6... | collective-permute-start | bytes 442376 | tf_op jit(solution)/shard_map/ppermute | solution.py:19
  14.5 22.0 %all-to-all-start = ((s32[32,1,96]{2,1,0:T(1,128)}), s32[32,1,96]{2,1,0:T(1,128)S(1)}, u32[]{:S(2)}, u32[]{:S(2)}) async-start(s32[32,1,96]{2,1,0:T(1,128)} %broadcast_in_dim.47), calls=%async_computation | async-start | bytes 32768 | tf_op jit(solution)/shard_map/all_to_all | solution.py:26
  28.4 2.7 %copy-start.2 = (bf16[384,1536]{1,0:T(8,128)(2,1)S(1)}, bf16[384,1536]{1,0:T(8,128)(2,1)}, u32[]{:S(2)}) copy-start(bf16[384,1536]{1,0:T(8,128)(2,1)} %param.15) | copy-start | bytes 3538948
  28.4 2.7 %copy-start.3 = (f32[384]{0:T(512)S(1)}, f32[384]{0:T(512)}, u32[]{:S(2)}) copy-start(f32[384]{0:T(512)} %param.17) | copy-start | bytes 4612
  38.1 65.6 %all-to-all-start.1 = ((bf16[32,96,384]{2,1,0:T(8,128)(2,1)}), bf16[32,96,384]{2,1,0:T(8,128)(2,1)}, u32[]{:S(2)}, u32[]{:S(2)}) async-start(bf16[32,96,384]{2,1,0:T(8,128)(2,1)} %broadcast_in_dim.48), calls=%async_computation.1 | async-start | bytes 4718592 | tf_op jit(solution)/shard_map/all_to_all | solution.py:26
  210.3 1.1 copy-start.1
where the time goes:
time: 215 us; the launch traced here: 213 us
  matrix products  77.8 us (36%)
  waiting for transfers between devices  54.9 us (26%)
  local copies, waits for them, and re-layouts  32.4 us (15%)
  starting transfers between devices  28.4 us (13%)
  other arithmetic  18.2 us (8%)
    all_to_all x2, waiting for transfers between devices, from_everyone(): return lax.all_to_all(copies, axis, split_axis=0, concat_axis=0, tiled=True)  54.9 us
    dot_general x16, matrix products, one_head(): jnp.einsum('qd,kd->qk', q_head, k_head, preferred_element_type=jnp.float32)  28 us
    dot_general x16, matrix products, one_head(): jnp.dot(weights.astype(jnp.bfloat16), v_head, preferred_element_type=jnp....  28 us
    all_to_all x2, starting transfers between devices, from_everyone(): return lax.all_to_all(copies, axis, split_axis=0, concat_axis=0, tiled=True)  21.6 us
    reshape x1, local copies, waits for them, and re-layouts, attend(): value_heads = jnp.transpose(values.reshape(count, HEADS, HD), (1, 0, 2))  12.1 us
    reshape x1, local copies, waits for them, and re-layouts, attend(): key_heads = jnp.transpose(keys.reshape(count, HEADS, HD), (1, 0, 2))  12 us
    reduce_sum x16, other arithmetic, one_head(): new_sum = run_sum * factor + jnp.sum(weights, axis=1)  9.07 us
    dot_general x1, matrix products, local(): jnp.dot(rows_in, w_value, preferred_element_type=jnp.float32)  8.02 us
  transfers between devices with their start and end apart: 4, of which 2 were waited for; matrix products, arithmetic and copies ran while one was open for 8% of the time, Pallas kernels for 0%

commit v1 on v0

v1 whole, which is shorter than its diff:
```python
import functools

import jax
import jax.numpy as jnp
from jax import lax
from jax.experimental import pallas as pl
from jax.experimental.pallas import tpu as pltpu
from jax.sharding import PartitionSpec as P

HEADS = 16
HD = 64
CAP = 96
ROWS = 3
GW = 64
C = 384
HID = 1536
TOK = ROWS * GW
UNIT = 2 * CAP
CHUNK = 4 * CAP
NCHUNK = 8
KS = 2 * CHUNK
QUADS = 4
QW = 256
MARK = 1024.0
NEG = -1e30

f32 = jnp.float32
bf16 = jnp.bfloat16
LAST = (((1,), (1,)), ((), ()))


def layer_norm(x):
    mean = jnp.mean(x, axis=-1, keepdims=True)
    centred = x - mean
    var = jnp.mean(centred * centred, axis=-1, keepdims=True)
    return centred * lax.rsqrt(var + 1e-06)


def matmul(a, b):
    return jnp.dot(a, b, preferred_element_type=f32)


def kernel(
    tokens, tissue, dw, w1, w2, scale, wq, wk, wv, wo, out,
    tok, tis, dwv, dwf, w1v, w2v, scv, wqv, wkv, wvv, wov,
    halo, thalo, ext, conv, sec, xbuf, k_all, v_all, qblk,
    s_ref, p_ref, m_ref, l_ref, a_ref, acc,
    load_sem, misc_s, misc_r, ring_s, ring_r, par_s, par_r,
):
    me = lax.axis_index("tile")
    core = lax.rem(me, 2)
    z = lax.rem(lax.div(me, 2), 8)
    y = lax.div(me, 16)
    partner = me + 1 - 2 * core
    zup = y * 16 + lax.rem(z + 1, 8) * 2 + core
    zdn = y * 16 + lax.rem(z + 7, 8) * 2 + core
    yoth = (1 - y) * 16 + z * 2 + core
    upper = lax.rem(me + 1, 32)
    lower = lax.rem(me + 31, 32)
    beyond = lower + core * (upper - lower)
    nxt = zup + core * (zdn - zup)
    half = pl.ds(pl.multiple_of(core * UNIT, UNIT), UNIT)

    pairs = [(tokens, tok), (tissue, tis), (dw, dwv), (w1, w1v), (w2, w2v), (scale, scv),
             (wq, wqv), (wk, wkv), (wv, wvv), (wo, wov)]
    loads = [pltpu.make_async_copy(a, b, load_sem.at[i]) for i, (a, b) in enumerate(pairs)]
    for load in loads:
        load.start()

    barrier = pltpu.get_barrier_semaphore()
    for other in (partner, zup, zdn, yoth, beyond):
        pl.semaphore_signal(barrier, inc=1, device_id={"tile": other},
                            device_id_type=pl.DeviceIdType.MESH)
    pl.semaphore_wait(barrier, 5)

    def remote(src, dst, send, recv, device):
        return pltpu.make_async_remote_copy(
            src_ref=src, dst_ref=dst, send_sem=send, recv_sem=recv,
            device_id={"tile": device}, device_id_type=pl.DeviceIdType.MESH)

    def misc(src, dst, i, device):
        return remote(src, dst, misc_s.at[i], misc_r.at[i], device)

    halos = [
        misc(tokens, halo.at[0], 0, upper), misc(tokens, halo.at[1], 1, lower),
        misc(tissue, thalo.at[0], 2, upper), misc(tissue, thalo.at[1], 3, lower),
    ]
    for copy in halos:
        copy.start()

    eye = lax.broadcasted_iota(jnp.int32, (GW, GW), 0) == lax.broadcasted_iota(jnp.int32, (GW, GW), 1)

    def column(row):
        return jnp.sum(jnp.where(eye, row.astype(f32), 0.0), axis=1, keepdims=True)

    col_ids = lax.broadcasted_iota(jnp.int32, (GW, 128), 0)

    def conv_pass(rows, first):
        @pl.loop(0, C // 128)
        def _(tile):
            lanes = pl.ds(pl.multiple_of(tile * 128, 128), 128)
            for r in range(ROWS):
                total = None
                for j in range(7):
                    part = None
                    for i in range(7):
                        if r + i in rows:
                            term = ext[r + i, :, lanes] * dwf[i, pl.ds(j, 1), lanes]
                            part = term if part is None else part + term
                    if part is None:
                        continue
                    s = j - 3
                    if s:
                        moved = pltpu.roll(part, (-s) % GW, 0)
                        inside = (col_ids + s >= 0) & (col_ids + s < GW)
                        part = jnp.where(inside, moved, 0.0)
                    total = part if total is None else total + part
                where = pl.ds(r * GW, GW)
                conv[where, lanes] = total if first else conv[where, lanes] + total

    for i in range(3):
        loads[i].wait()
    dwf[...] = dwv[...].astype(f32)
    for r in range(ROWS):
        ext[3 + r] = tok[r].astype(f32) * column(tis[r : r + 1, :])
    conv_pass((3, 4, 5), True)
    for copy in halos:
        copy.wait_recv()
    has_low = jnp.where(me > 0, 1.0, 0.0)
    has_high = jnp.where(me < 31, 1.0, 0.0)
    for r in range(ROWS):
        ext[r] = halo[0, r].astype(f32) * (column(thalo[0, r : r + 1, :]) * has_low)
        ext[6 + r] = halo[1, r].astype(f32) * (column(thalo[1, r : r + 1, :]) * has_high)
    conv_pass((0, 1, 2, 6, 7, 8), False)

    normed1 = layer_norm(conv[...]).astype(bf16)
    for i in range(3, 6):
        loads[i].wait()
    branch = None
    for n in range(3):
        cut = slice(n * 512, (n + 1) * 512)
        h = matmul(normed1, w1v[:, cut])
        h = (0.5 * h * (1.0 + lax.erf(h * 0.7071067811865476))).astype(bf16)
        part = matmul(h, w2v[cut, :])
        branch = part if branch is None else branch + part
    masked = ext[3:6].reshape(TOK, C)
    section = (masked + scv[...][None, :] * branch).astype(bf16)
    sec[...] = section
    normed2 = layer_norm(section.astype(f32)).astype(bf16)

    flags = tis[...].astype(f32)
    before = lax.broadcasted_iota(jnp.int32, (GW, GW), 0) < lax.broadcasted_iota(jnp.int32, (GW, GW), 1)
    rank = matmul(flags.astype(bf16), jnp.where(before, 1.0, 0.0).astype(bf16))
    counts = jnp.sum(flags, axis=1, keepdims=True)
    slot = lax.broadcasted_iota(jnp.int32, (CAP, GW), 0).astype(f32)
    x = jnp.zeros((CAP, C), f32)
    offset = jnp.zeros((1, 1), f32)
    for r in range(ROWS):
        pick = (slot == rank[r : r + 1, :] + offset) & (flags[r : r + 1, :] > 0)
        x = x + matmul(jnp.where(pick, 1.0, 0.0).astype(bf16), normed2[r * GW : (r + 1) * GW, :])
        offset = offset + counts[r : r + 1, :]
    empty = (lax.broadcasted_iota(jnp.int32, (CAP, C), 0).astype(f32) >= offset) & (
        lax.broadcasted_iota(jnp.int32, (CAP, C), 1) == 0)
    x = jnp.where(empty, MARK, x).astype(bf16)

    own = xbuf.at[0, pl.ds(pl.multiple_of(core * CAP, CAP), CAP)]
    far = xbuf.at[0, pl.ds(pl.multiple_of(UNIT + core * CAP, CAP), CAP)]
    xbuf[0, pl.ds(pl.multiple_of(core * CAP, CAP), CAP), :] = x
    own_copy = misc(own, own, 4, partner)
    far_copy = misc(own, far, 5, yoth)
    far_share = misc(far, far, 6, partner)
    own_copy.start()
    far_copy.start()

    def ring(src, dst):
        return remote(xbuf.at[src, half], xbuf.at[dst, half], ring_s.at[dst], ring_r.at[dst], nxt)

    def share(c):
        return remote(xbuf.at[c, half], xbuf.at[c, half], par_s.at[c], par_r.at[c], partner)

    def first_ring(unit, dst):
        return remote(xbuf.at[0, pl.ds(unit * UNIT, UNIT)], xbuf.at[dst, half],
                      ring_s.at[dst], ring_r.at[dst], nxt)

    own_copy.wait_recv()
    first_ring(0, 1).start()

    loads[6].wait()
    lane = lax.broadcasted_iota(jnp.int32, (TOK, QW), 1)
    for g in range(QUADS):
        query = matmul(normed2, wqv[:, g * QW : (g + 1) * QW]).astype(bf16).astype(f32) * 0.125
        for h in range(4):
            mine = (lane >= h * HD) & (lane < (h + 1) * HD)
            qblk[g, h * TOK : (h + 1) * TOK, :] = jnp.where(mine, query, 0.0).astype(bf16)
    m_ref[...] = jnp.full(m_ref.shape, NEG, f32)
    l_ref[...] = jnp.zeros(l_ref.shape, f32)
    acc[...] = jnp.zeros(acc.shape, f32)

    far_copy.wait_recv()
    far_share.start()
    far_share.wait_recv()
    first_ring(1, 2).start()
    loads[7].wait()
    loads[8].wait()

    first_lane = jnp.where(lax.broadcasted_iota(jnp.int32, (8, C), 1) == 0, 1.0, 0.0).astype(bf16)

    def project(c):
        rows = pl.ds(pl.multiple_of(c * CHUNK, CHUNK), CHUNK)
        xc = xbuf[c]
        for n in range(4):
            cut = slice(n * 256, (n + 1) * 256)
            k_all[rows, cut] = matmul(xc, wkv[:, cut]).astype(bf16)
            v_all[rows, cut] = matmul(xc, wvv[:, cut]).astype(bf16)

    project(0)
    ring(0, 1).wait_recv()
    ring(1, 3).start()
    share(1).start()
    share(1).wait_recv()
    project(1)

    half_lane = lax.broadcasted_iota(jnp.int32, (TOK, 128), 1) < HD

    def scores(p, g):
        rows = pl.ds(pl.multiple_of(p * KS, KS), KS)
        s_ref[g % 2] = lax.dot_general(
            qblk[g], k_all[rows, g * QW : (g + 1) * QW], LAST, preferred_element_type=f32)

    def attend(p, g, shift):
        at = g % 2
        tiles = range(KS // 128)
        for r in range(0, 4 * TOK, 32):
            rs = slice(r, r + 32)
            st = [
                (s_ref[at, rs, t * 128 : (t + 1) * 128].reshape(4, 8, 128)
                 + shift[:, t * 128 : (t + 1) * 128][None]).reshape(32, 128)
                for t in tiles
            ]
            top = functools.reduce(jnp.maximum, st)
            old = m_ref[g, rs, :]
            new = jnp.maximum(old, jnp.max(top, axis=1, keepdims=True))
            factor = jnp.exp(old - new)
            m_ref[g, rs, :] = new
            a_ref[at, rs, :] = factor
            total = None
            for t in tiles:
                weight = jnp.exp(st[t] - new)
                p_ref[at, rs, t * 128 : (t + 1) * 128] = weight.astype(bf16)
                total = weight if total is None else total + weight
            l_ref[g, rs, :] = l_ref[g, rs, :] * factor + total
        rows = pl.ds(pl.multiple_of(p * KS, KS), KS)
        o = matmul(p_ref[at], v_all[rows, g * QW : (g + 1) * QW])
        for t in range(2):
            a, b = slice(2 * t * TOK, (2 * t + 1) * TOK), slice((2 * t + 1) * TOK, (2 * t + 2) * TOK)
            cut = slice(t * 128, (t + 1) * 128)
            o_t = jnp.where(half_lane, o[a, cut], o[b, cut])
            f_t = jnp.where(half_lane, a_ref[at, a, :], a_ref[at, b, :])
            dst = slice(g * QW + t * 128, g * QW + (t + 1) * 128)
            acc[:, dst] = acc[:, dst] * f_t + o_t

    @pl.loop(0, 4)
    def _(p):
        even, odd = 2 * p + 2, 2 * p + 3
        marks = [
            lax.dot_general(first_lane, xbuf[2 * p + i], LAST, preferred_element_type=f32) for i in range(2)
        ]
        shift = jnp.where(jnp.concatenate(marks, axis=1) > 0.5 * MARK, NEG, 0.0)
        scores(p, 0)
        attend(p, 0, shift)

        @pl.when(p < 3)
        def _():
            ring(even, even).wait_recv()
            share(even).start()

        @pl.when(p < 2)
        def _():
            ring(even, even + 2).start()

        @pl.when(p == 2)
        def _():
            ring(5 + core, 7).start()

        scores(p, 1)
        attend(p, 1, shift)

        @pl.when(p < 3)
        def _():
            ring(odd, odd).wait_recv()
            share(odd).start()

        @pl.when(p == 0)
        def _():
            ring(odd, odd + 2).start()

        @pl.when(p < 3)
        def _():
            share(even).wait_recv()
            project(even)

        scores(p, 2)
        attend(p, 2, shift)

        @pl.when(p < 3)
        def _():
            share(odd).wait_recv()
            project(odd)

        scores(p, 3)
        attend(p, 3, shift)

    loads[9].wait()
    result = sec[...].astype(f32)
    for g in range(QUADS):
        parts = []
        for t in range(2):
            a, b = slice(2 * t * TOK, (2 * t + 1) * TOK), slice((2 * t + 1) * TOK, (2 * t + 2) * TOK)
            total_a = jnp.sum(l_ref[g, a, :], axis=1, keepdims=True)
            total_b = jnp.sum(l_ref[g, b, :], axis=1, keepdims=True)
            dst = slice(g * QW + t * 128, g * QW + (t + 1) * 128)
            parts.append((acc[:, dst] / jnp.where(half_lane, total_a, total_b)).astype(bf16))
        result = result + matmul(jnp.concatenate(parts, axis=1), wov[g * QW : (g + 1) * QW, :])
    out[...] = result.astype(bf16).reshape(ROWS, GW, C)

    for copy in halos + [own_copy, far_copy, far_share]:
        copy.wait_send()
    for c in range(1, NCHUNK):
        ring(c, c).wait_send()
        share(c).wait_send()


def local(tokens, tissue, dw_kernel, w_fc1, w_fc2, layer_scale, w_query, w_key, w_value, w_out):
    vmem, sem = pltpu.VMEM, pltpu.SemaphoreType.DMA
    return pl.pallas_call(
        kernel,
        out_shape=jax.ShapeDtypeStruct((ROWS, GW, C), bf16),
        in_specs=[pl.BlockSpec(memory_space=pl.ANY)] * 10,
        out_specs=pl.BlockSpec(memory_space=pltpu.VMEM),
        scratch_shapes=[
            vmem((ROWS, GW, C), bf16), vmem((ROWS, GW), jnp.int32),
            vmem((7, 7, C), bf16), vmem((7, 7, C), f32),
            vmem((C, HID), bf16), vmem((HID, C), bf16), vmem((C,), f32),
            vmem((C, 1024), bf16), vmem((C, 1024), bf16), vmem((C, 1024), bf16), vmem((1024, C), bf16),
            vmem((2, ROWS, GW, C), bf16), vmem((2, ROWS, GW), jnp.int32),
            vmem((9, GW, C), f32), vmem((TOK, C), f32), vmem((TOK, C), bf16),
            vmem((NCHUNK, CHUNK, C), bf16),
            vmem((NCHUNK * CHUNK, 1024), bf16), vmem((NCHUNK * CHUNK, 1024), bf16),
            vmem((QUADS, 4 * TOK, QW), bf16),
            vmem((2, 4 * TOK, KS), f32), vmem((2, 4 * TOK, KS), bf16),
            vmem((QUADS, 4 * TOK, 128), f32), vmem((QUADS, 4 * TOK, 128), f32),
            vmem((2, 4 * TOK, 128), f32), vmem((TOK, 1024), f32),
            sem((10,)), sem((7,)), sem((7,)), sem((NCHUNK,)), sem((NCHUNK,)), sem((NCHUNK,)), sem((NCHUNK,)),
        ],
        compiler_params=pltpu.CompilerParams(
            collective_id=0, has_side_effects=True, vmem_limit_bytes=60 << 20),
        name="block",
    )(tokens, tissue, dw_kernel, w_fc1, w_fc2, layer_scale, w_query, w_key, w_value, w_out)


def solution(mesh):
    spec = P(("slide", "tile"), None, None)
    in_specs = (spec, P(("slide", "tile"), None)) + (P(),) * 8
    return jax.shard_map(local, mesh=mesh, in_specs=in_specs, out_specs=spec, check_vma=False)
```

time: 215 us -> 65 us (0.30)
  matrix products: 77.8 us -> 0 us
  Pallas kernels: 0 us -> 62.9 us
  waiting for transfers between devices: 54.9 us -> 0 us
  local copies, waits for them, and re-layouts: 32.4 us -> 1.59 us
  starting transfers between devices: 28.4 us -> 0 us
  other arithmetic: 18.2 us -> 0 us
    dot_general x37 -> x0, matrix products: 77.8 us -> none  [the longest x16 28 us: one_head(): jnp.einsum('qd,kd->qk', q_head, k_head, preferred_element_type=jnp.float32)]
    pallas_call x0 -> x1, Pallas kernels: none -> 62.9 us  [local(): pl.pallas_call(kernel, out_shape=jax.ShapeDtypeStruct((ROWS, GW, C), bf16...]
    all_to_all x2 -> x0, waiting for transfers between devices: 54.9 us -> none  [from_everyone(): return lax.all_to_all(copies, axis, split_axis=0, concat_axis=0, tiled=True)]
    reshape x3 -> x0, local copies, waits for them, and re-layouts: 24.9 us -> none  [the longest x1 12.1 us: attend(): value_heads = jnp.transpose(values.reshape(count, HEADS, HD), (1, 0, 2))]
    all_to_all x2 -> x0, starting transfers between devices: 21.6 us -> none  [from_everyone(): return lax.all_to_all(copies, axis, split_axis=0, concat_axis=0, tiled=True)]
    reduce_sum x19 -> x0, other arithmetic: 11.6 us -> none  [the longest x16 9.07 us: one_head(): new_sum = run_sum * factor + jnp.sum(weights, axis=1)]
    ppermute x2 -> x0, starting transfers between devices: 6.84 us -> none  [the longest x1 4.92 us: padded_2(): lax.ppermute(lax.slice_in_dim(block, block.shape[dim] - width, None, axis...]
    sort x1 -> x0, other arithmetic: 3.17 us -> none  [local(): order = jnp.argsort(1 - flags, stable=True)[:CAP]]
  transfers between devices with their start and end apart: 4 -> 0, of which waited for: 2 -> 0; matrix products, arithmetic and copies ran while one was open for 8% -> 0% of each run, Pallas kernels for 0% -> 0%
where the time goes in v1:
time: 65 us; the launch traced here: 64.4 us
  Pallas kernels  62.9 us (97%)
  local copies, waits for them, and re-layouts  1.59 us (2%)
    pallas_call x1, Pallas kernels, local(): pl.pallas_call(kernel, out_shape=jax.ShapeDtypeStruct((ROWS, GW, C), bf16...  62.9 us
    unnamed x1, local copies, waits for them, and re-layouts  1.59 us

profile of v1, /device:TPU:1, one launch (start us, length us, event | category | flops | bytes accessed | tf_op | source)
XLA Modules:
  0.0 64.4 jit_solution(11838305265420495612)
XLA Ops:
  0.0 62.9 %block.1 = bf16[3,64,384]{2,1,0:T(8,128)(2,1)} custom-call(bf16[3,64,384]{2,1,0:T(8,128)(2,1)} %tokens.1, s32[3,64]{1,0:T(4,128)} %tissue.1, bf16[7,7,384]{2,1,0:T(8,128)(2,1)} %dw.1, bf16[384,1536]{1,0:T(8,128)(2,1)} %w1.1, bf16[1536,384]{1,0:T(8,128)(2,1)} %w2.1, f32[384]{0:T(512)} %scale.1, bf16[384,1024]{1,0:T(8,128)(2,1)} %wq.1, bf16[384,1024]{1,0:T(8,128)(2,1)} %wk.1, ...), custom_call_target="tpu_custom_call" | custom-call | tf_op jit(solution)/shard_map/block/pallas_call | solution.py:335
  62.9 1.6 %copy.12 = bf16[3,64,384]{2,1,0:T(8,128)(2,1)} copy(bf16[3,64,384]{2,1,0:T(8,128)(2,1)} %block.1) | data formatting | bytes 294912

commit v2 on v1

--- a/solution.py
+++ b/solution.py
@@ -205,20 +205,19 @@
 
     first_lane = jnp.where(lax.broadcasted_iota(jnp.int32, (8, C), 1) == 0, 1.0, 0.0).astype(bf16)
 
-    def project(c):
-        rows = pl.ds(pl.multiple_of(c * CHUNK, CHUNK), CHUNK)
-        xc = xbuf[c]
+    def project(p):
+        rows = pl.ds(pl.multiple_of(p * KS, KS), KS)
+        xc = xbuf[pl.ds(2 * p, 2)].reshape(KS, C)
         for n in range(4):
             cut = slice(n * 256, (n + 1) * 256)
             k_all[rows, cut] = matmul(xc, wkv[:, cut]).astype(bf16)
             v_all[rows, cut] = matmul(xc, wvv[:, cut]).astype(bf16)
 
-    project(0)
     ring(0, 1).wait_recv()
     ring(1, 3).start()
     share(1).start()
     share(1).wait_recv()
-    project(1)
+    project(0)
 
     half_lane = lax.broadcasted_iota(jnp.int32, (TOK, 128), 1) < HD
 
@@ -259,56 +258,46 @@
             dst = slice(g * QW + t * 128, g * QW + (t + 1) * 128)
             acc[:, dst] = acc[:, dst] * f_t + o_t
 
-    @pl.loop(0, 4)
-    def _(p):
-        even, odd = 2 * p + 2, 2 * p + 3
+    def mask(p):
         marks = [
             lax.dot_general(first_lane, xbuf[2 * p + i], LAST, preferred_element_type=f32) for i in range(2)
         ]
-        shift = jnp.where(jnp.concatenate(marks, axis=1) > 0.5 * MARK, NEG, 0.0)
-        scores(p, 0)
+        return jnp.where(jnp.concatenate(marks, axis=1) > 0.5 * MARK, NEG, 0.0)
+
+    scores(0, 0)
+
+    @pl.loop(0, 3)
+    def _(p):
+        even, odd = 2 * p + 2, 2 * p + 3
+        last = lax.div(p, 2)
+        shift = mask(p)
+        scores(p, 1)
         attend(p, 0, shift)
-
-        @pl.when(p < 3)
-        def _():
-            ring(even, even).wait_recv()
-            share(even).start()
-
-        @pl.when(p < 2)
-        def _():
-            ring(even, even + 2).start()
-
-        @pl.when(p == 2)
-        def _():
-            ring(5 + core, 7).start()
-
-        scores(p, 1)
+        ring(even, even).wait_recv()
+        share(even).start()
+        ring(even + last * (core - 1), even + 2 - last).start()
+        scores(p, 2)
         attend(p, 1, shift)
-
-        @pl.when(p < 3)
-        def _():
-            ring(odd, odd).wait_recv()
-            share(odd).start()
+        ring(odd, odd).wait_recv()
+        share(odd).start()
 
         @pl.when(p == 0)
         def _():
             ring(odd, odd + 2).start()
 
-        @pl.when(p < 3)
-        def _():
-            share(even).wait_recv()
-            project(even)
-
-        scores(p, 2)
+        scores(p, 3)
         attend(p, 2, shift)
-
-        @pl.when(p < 3)
-        def _():
-            share(odd).wait_recv()
-            project(odd)
-
-        scores(p, 3)
+        share(even).wait_recv()
+        share(odd).wait_recv()
+        project(p + 1)
+        scores(p + 1, 0)
         attend(p, 3, shift)
+
+    shift = mask(3)
+    for g in range(QUADS):
+        if g < 3:
+            scores(3, g + 1)
+        attend(3, g, shift)
 
     loads[9].wait()
     result = sec[...].astype(f32)

time: 65 us -> 58.7 us (0.903)
  Pallas kernels: 62.9 us -> 57.1 us
    pallas_call x1, Pallas kernels: 62.9 us -> 57.1 us  [local(): pl.pallas_call(kernel, out_shape=jax.ShapeDtypeStruct((ROWS, GW, C), bf16...]
where the time goes in v2:
time: 58.7 us; the launch traced here: 58.6 us
  Pallas kernels  57.1 us (97%)
  local copies, waits for them, and re-layouts  1.59 us (3%)
    pallas_call x1, Pallas kernels, local(): pl.pallas_call(kernel, out_shape=jax.ShapeDtypeStruct((ROWS, GW, C), bf16...  57.1 us
    unnamed x1, local copies, waits for them, and re-layouts  1.59 us

profile of v2, /device:TPU:1, one launch (start us, length us, event | category | flops | bytes accessed | tf_op | source)
XLA Modules:
  0.0 58.6 jit_solution(15756890111108542381)
XLA Ops:
  0.0 57.1 %block.1 = bf16[3,64,384]{2,1,0:T(8,128)(2,1)} custom-call(bf16[3,64,384]{2,1,0:T(8,128)(2,1)} %tokens.1, s32[3,64]{1,0:T(4,128)} %tissue.1, bf16[7,7,384]{2,1,0:T(8,128)(2,1)} %dw.1, bf16[384,1536]{1,0:T(8,128)(2,1)} %w1.1, bf16[1536,384]{1,0:T(8,128)(2,1)} %w2.1, f32[384]{0:T(512)} %scale.1, bf16[384,1024]{1,0:T(8,128)(2,1)} %wq.1, bf16[384,1024]{1,0:T(8,128)(2,1)} %wk.1, ...), custom_call_target="tpu_custom_call" | custom-call | tf_op jit(solution)/shard_map/block/pallas_call | solution.py:324
  57.1 1.6 %copy.12 = bf16[3,64,384]{2,1,0:T(8,128)(2,1)} copy(bf16[3,64,384]{2,1,0:T(8,128)(2,1)} %block.1) | data formatting | bytes 294912

commit v3 on v2

--- a/solution.py
+++ b/solution.py
@@ -19,8 +19,9 @@
 CHUNK = 4 * CAP
 NCHUNK = 8
 KS = 2 * CHUNK
-QUADS = 4
+GROUPS = 4
 QW = 256
+HALF = 512
 MARK = 1024.0
 NEG = -1e30
 
@@ -43,8 +44,8 @@
 def kernel(
     tokens, tissue, dw, w1, w2, scale, wq, wk, wv, wo, out,
     tok, tis, dwv, dwf, w1v, w2v, scv, wqv, wkv, wvv, wov,
-    halo, thalo, ext, conv, sec, xbuf, k_all, v_all, qblk,
-    s_ref, p_ref, m_ref, l_ref, a_ref, acc,
+    halo, thalo, ext, conv, sec, n2buf, xbuf, k_all, v_all, qblk,
+    s_ref, p_ref, m_ref, l_ref, a_ref, acc, att_out, att_in,
     load_sem, misc_s, misc_r, ring_s, ring_r, par_s, par_r,
 ):
     me = lax.axis_index("tile")
@@ -61,8 +62,11 @@
     nxt = zup + core * (zdn - zup)
     half = pl.ds(pl.multiple_of(core * UNIT, UNIT), UNIT)
 
+    mine = pl.ds(pl.multiple_of(core * HALF, HALF), HALF)
+    theirs = pl.ds(pl.multiple_of((1 - core) * HALF, HALF), HALF)
     pairs = [(tokens, tok), (tissue, tis), (dw, dwv), (w1, w1v), (w2, w2v), (scale, scv),
-             (wq, wqv), (wk, wkv), (wv, wvv), (wo, wov)]
+             (wq.at[:, mine], wqv), (wk.at[:, mine], wkv), (wv.at[:, mine], wvv),
+             (wo.at[mine], wov.at[0]), (wo.at[theirs], wov.at[1])]
     loads = [pltpu.make_async_copy(a, b, load_sem.at[i]) for i, (a, b) in enumerate(pairs)]
     for load in loads:
         load.start()
@@ -147,6 +151,7 @@
     section = (masked + scv[...][None, :] * branch).astype(bf16)
     sec[...] = section
     normed2 = layer_norm(section.astype(f32)).astype(bf16)
+    n2buf[1] = normed2
 
     flags = tis[...].astype(f32)
     before = lax.broadcasted_iota(jnp.int32, (GW, GW), 0) < lax.broadcasted_iota(jnp.int32, (GW, GW), 1)
@@ -169,8 +174,11 @@
     own_copy = misc(own, own, 4, partner)
     far_copy = misc(own, far, 5, yoth)
     far_share = misc(far, far, 6, partner)
+    n2_copy = misc(n2buf.at[1], n2buf.at[0], 7, partner)
+    att_copy = misc(att_out, att_in, 8, partner)
     own_copy.start()
     far_copy.start()
+    n2_copy.start()
 
     def ring(src, dst):
         return remote(xbuf.at[src, half], xbuf.at[dst, half], ring_s.at[dst], ring_r.at[dst], nxt)
@@ -187,17 +195,25 @@
 
     loads[6].wait()
     lane = lax.broadcasted_iota(jnp.int32, (TOK, QW), 1)
-    for g in range(QUADS):
-        query = matmul(normed2, wqv[:, g * QW : (g + 1) * QW]).astype(bf16).astype(f32) * 0.125
+
+    def queries(group, normed):
+        cut = slice((group % 2) * QW, (group % 2 + 1) * QW)
+        query = matmul(normed, wqv[:, cut]).astype(bf16).astype(f32) * 0.125
         for h in range(4):
-            mine = (lane >= h * HD) & (lane < (h + 1) * HD)
-            qblk[g, h * TOK : (h + 1) * TOK, :] = jnp.where(mine, query, 0.0).astype(bf16)
+            inside = (lane >= h * HD) & (lane < (h + 1) * HD)
+            qblk[group, h * TOK : (h + 1) * TOK, :] = jnp.where(inside, query, 0.0).astype(bf16)
+
+    for group in (2, 3):
+        queries(group, normed2)
     m_ref[...] = jnp.full(m_ref.shape, NEG, f32)
     l_ref[...] = jnp.zeros(l_ref.shape, f32)
     acc[...] = jnp.zeros(acc.shape, f32)
 
     far_copy.wait_recv()
     far_share.start()
+    n2_copy.wait_recv()
+    for group in (0, 1):
+        queries(group, n2buf[0])
     far_share.wait_recv()
     first_ring(1, 2).start()
     loads[7].wait()
@@ -208,7 +224,7 @@
     def project(p):
         rows = pl.ds(pl.multiple_of(p * KS, KS), KS)
         xc = xbuf[pl.ds(2 * p, 2)].reshape(KS, C)
-        for n in range(4):
+        for n in range(2):
             cut = slice(n * 256, (n + 1) * 256)
             k_all[rows, cut] = matmul(xc, wkv[:, cut]).astype(bf16)
             v_all[rows, cut] = matmul(xc, wvv[:, cut]).astype(bf16)
@@ -224,7 +240,7 @@
     def scores(p, g):
         rows = pl.ds(pl.multiple_of(p * KS, KS), KS)
         s_ref[g % 2] = lax.dot_general(
-            qblk[g], k_all[rows, g * QW : (g + 1) * QW], LAST, preferred_element_type=f32)
+            qblk[g], k_all[rows, (g % 2) * QW : (g % 2 + 1) * QW], LAST, preferred_element_type=f32)
 
     def attend(p, g, shift):
         at = g % 2
@@ -249,14 +265,14 @@
                 total = weight if total is None else total + weight
             l_ref[g, rs, :] = l_ref[g, rs, :] * factor + total
         rows = pl.ds(pl.multiple_of(p * KS, KS), KS)
-        o = matmul(p_ref[at], v_all[rows, g * QW : (g + 1) * QW])
+        o = matmul(p_ref[at], v_all[rows, (g % 2) * QW : (g % 2 + 1) * QW])
         for t in range(2):
             a, b = slice(2 * t * TOK, (2 * t + 1) * TOK), slice((2 * t + 1) * TOK, (2 * t + 2) * TOK)
             cut = slice(t * 128, (t + 1) * 128)
             o_t = jnp.where(half_lane, o[a, cut], o[b, cut])
             f_t = jnp.where(half_lane, a_ref[at, a, :], a_ref[at, b, :])
-            dst = slice(g * QW + t * 128, g * QW + (t + 1) * 128)
-            acc[:, dst] = acc[:, dst] * f_t + o_t
+            dst = slice((g % 2) * QW + t * 128, (g % 2) * QW + (t + 1) * 128)
+            acc[g // 2, :, dst] = acc[g // 2, :, dst] * f_t + o_t
 
     def mask(p):
         marks = [
@@ -293,26 +309,36 @@
         scores(p + 1, 0)
         attend(p, 3, shift)
 
+    def attended(who):
+        parts = []
+        for g in (2 * who, 2 * who + 1):
+            for t in range(2):
+                a, b = slice(2 * t * TOK, (2 * t + 1) * TOK), slice((2 * t + 1) * TOK, (2 * t + 2) * TOK)
+                total_a = jnp.sum(l_ref[g, a, :], axis=1, keepdims=True)
+                total_b = jnp.sum(l_ref[g, b, :], axis=1, keepdims=True)
+                dst = slice((g % 2) * QW + t * 128, (g % 2) * QW + (t + 1) * 128)
+                parts.append((acc[who, :, dst] / jnp.where(half_lane, total_a, total_b)).astype(bf16))
+        return jnp.concatenate(parts, axis=1)
+
     shift = mask(3)
-    for g in range(QUADS):
-        if g < 3:
-            scores(3, g + 1)
-        attend(3, g, shift)
+    scores(3, 1)
+    attend(3, 0, shift)
+    scores(3, 2)
+    attend(3, 1, shift)
+    att_out[...] = attended(0)
+    att_copy.start()
+    scores(3, 3)
+    attend(3, 2, shift)
+    attend(3, 3, shift)
 
     loads[9].wait()
-    result = sec[...].astype(f32)
-    for g in range(QUADS):
-        parts = []
-        for t in range(2):
-            a, b = slice(2 * t * TOK, (2 * t + 1) * TOK), slice((2 * t + 1) * TOK, (2 * t + 2) * TOK)
-            total_a = jnp.sum(l_ref[g, a, :], axis=1, keepdims=True)
-            total_b = jnp.sum(l_ref[g, b, :], axis=1, keepdims=True)
-            dst = slice(g * QW + t * 128, g * QW + (t + 1) * 128)
-            parts.append((acc[:, dst] / jnp.where(half_lane, total_a, total_b)).astype(bf16))
-        result = result + matmul(jnp.concatenate(parts, axis=1), wov[g * QW : (g + 1) * QW, :])
+    loads[10].wait()
+    result = sec[...].astype(f32) + matmul(attended(1), wov[0])
+    att_copy.wait_recv()
+    result = result + matmul(att_in[...], wov[1])
     out[...] = result.astype(bf16).reshape(ROWS, GW, C)
 
-    for copy in halos + [own_copy, far_copy, far_share]:
+    for copy in halos + [own_copy, far_copy, far_share, n2_copy, att_copy]:
         copy.wait_send()
     for c in range(1, NCHUNK):
         ring(c, c).wait_send()
@@ -330,16 +356,17 @@
             vmem((ROWS, GW, C), bf16), vmem((ROWS, GW), jnp.int32),
             vmem((7, 7, C), bf16), vmem((7, 7, C), f32),
             vmem((C, HID), bf16), vmem((HID, C), bf16), vmem((C,), f32),
-            vmem((C, 1024), bf16), vmem((C, 1024), bf16), vmem((C, 1024), bf16), vmem((1024, C), bf16),
+            vmem((C, HALF), bf16), vmem((C, HALF), bf16), vmem((C, HALF), bf16), vmem((2, HALF, C), bf16),
             vmem((2, ROWS, GW, C), bf16), vmem((2, ROWS, GW), jnp.int32),
             vmem((9, GW, C), f32), vmem((TOK, C), f32), vmem((TOK, C), bf16),
-            vmem((NCHUNK, CHUNK, C), bf16),
-            vmem((NCHUNK * CHUNK, 1024), bf16), vmem((NCHUNK * CHUNK, 1024), bf16),
-            vmem((QUADS, 4 * TOK, QW), bf16),
+            vmem((2, TOK, C), bf16), vmem((NCHUNK, CHUNK, C), bf16),
+            vmem((NCHUNK * CHUNK, HALF), bf16), vmem((NCHUNK * CHUNK, HALF), bf16),
+            vmem((GROUPS, 4 * TOK, QW), bf16),
             vmem((2, 4 * TOK, KS), f32), vmem((2, 4 * TOK, KS), bf16),
-            vmem((QUADS, 4 * TOK, 128), f32), vmem((QUADS, 4 * TOK, 128), f32),
-            vmem((2, 4 * TOK, 128), f32), vmem((TOK, 1024), f32),
-            sem((10,)), sem((7,)), sem((7,)), sem((NCHUNK,)), sem((NCHUNK,)), sem((NCHUNK,)), sem((NCHUNK,)),
+            vmem((GROUPS, 4 * TOK, 128), f32), vmem((GROUPS, 4 * TOK, 128), f32),
+            vmem((2, 4 * TOK, 128), f32), vmem((2, TOK, HALF), f32),
+            vmem((TOK, HALF), bf16), vmem((TOK, HALF), bf16),
+            sem((11,)), sem((9,)), sem((9,)), sem((NCHUNK,)), sem((NCHUNK,)), sem((NCHUNK,)), sem((NCHUNK,)),
         ],
         compiler_params=pltpu.CompilerParams(
             collective_id=0, has_side_effects=True, vmem_limit_bytes=60 << 20),

time: 58.7 us -> 55.9 us (0.952)
  Pallas kernels: 57.1 us -> 54.2 us
    pallas_call x1, Pallas kernels: 57.1 us -> 54.2 us  [local(): pl.pallas_call(kernel, out_shape=jax.ShapeDtypeStruct((ROWS, GW, C), bf16...]
where the time goes in v3:
time: 55.9 us; the launch traced here: 55.8 us
  Pallas kernels  54.2 us (97%)
  local copies, waits for them, and re-layouts  1.59 us (3%)
    pallas_call x1, Pallas kernels, local(): pl.pallas_call(kernel, out_shape=jax.ShapeDtypeStruct((ROWS, GW, C), bf16...  54.2 us
    unnamed x1, local copies, waits for them, and re-layouts  1.59 us

profile of v3, /device:TPU:1, one launch (start us, length us, event | category | flops | bytes accessed | tf_op | source)
XLA Modules:
  0.0 55.8 jit_solution(2121243513289840864)
XLA Ops:
  0.0 54.2 %block.1 = bf16[3,64,384]{2,1,0:T(8,128)(2,1)} custom-call(bf16[3,64,384]{2,1,0:T(8,128)(2,1)} %tokens.1, s32[3,64]{1,0:T(4,128)} %tissue.1, bf16[7,7,384]{2,1,0:T(8,128)(2,1)} %dw.1, bf16[384,1536]{1,0:T(8,128)(2,1)} %w1.1, bf16[1536,384]{1,0:T(8,128)(2,1)} %w2.1, f32[384]{0:T(512)} %scale.1, bf16[384,1024]{1,0:T(8,128)(2,1)} %wq.1, bf16[384,1024]{1,0:T(8,128)(2,1)} %wk.1, ...), custom_call_target="tpu_custom_call" | custom-call | tf_op jit(solution)/shard_map/block/pallas_call | solution.py:350
  54.2 1.6 %copy.12 = bf16[3,64,384]{2,1,0:T(8,128)(2,1)} copy(bf16[3,64,384]{2,1,0:T(8,128)(2,1)} %block.1) | data formatting | bytes 294912

commit v4 on v3

--- a/solution.py
+++ b/solution.py
@@ -59,8 +59,7 @@
     upper = lax.rem(me + 1, 32)
     lower = lax.rem(me + 31, 32)
     beyond = lower + core * (upper - lower)
-    nxt = zup + core * (zdn - zup)
-    half = pl.ds(pl.multiple_of(core * UNIT, UNIT), UNIT)
+    along = (zup, zdn)
 
     mine = pl.ds(pl.multiple_of(core * HALF, HALF), HALF)
     theirs = pl.ds(pl.multiple_of((1 - core) * HALF, HALF), HALF)
@@ -68,7 +67,7 @@
              (wq.at[:, mine], wqv), (wk.at[:, mine], wkv), (wv.at[:, mine], wvv),
              (wo.at[mine], wov.at[0]), (wo.at[theirs], wov.at[1])]
     loads = [pltpu.make_async_copy(a, b, load_sem.at[i]) for i, (a, b) in enumerate(pairs)]
-    for load in loads:
+    for load in loads[:3]:
         load.start()
 
     barrier = pltpu.get_barrier_semaphore()
@@ -91,6 +90,8 @@
     ]
     for copy in halos:
         copy.start()
+    for load in loads[3:]:
+        load.start()
 
     eye = lax.broadcasted_iota(jnp.int32, (GW, GW), 0) == lax.broadcasted_iota(jnp.int32, (GW, GW), 1)
 
@@ -176,22 +177,26 @@
     far_share = misc(far, far, 6, partner)
     n2_copy = misc(n2buf.at[1], n2buf.at[0], 7, partner)
     att_copy = misc(att_out, att_in, 8, partner)
+
+    def block(c, way):
+        return xbuf.at[c, pl.ds(pl.multiple_of(way * UNIT + core * CAP, CAP), CAP)]
+
+    def hop(src, way, dst):
+        at = way * NCHUNK + dst
+        return remote(src, block(dst, way), ring_s.at[at], ring_r.at[at], along[way])
+
+    def ring(way, src, dst):
+        return hop(block(src, way), way, dst)
+
+    def share(way, c):
+        at = way * NCHUNK + c
+        return remote(block(c, way), block(c, way), par_s.at[at], par_r.at[at], partner)
+
+    for way in range(2):
+        hop(own, way, 1).start()
+    far_copy.start()
     own_copy.start()
-    far_copy.start()
     n2_copy.start()
-
-    def ring(src, dst):
-        return remote(xbuf.at[src, half], xbuf.at[dst, half], ring_s.at[dst], ring_r.at[dst], nxt)
-
-    def share(c):
-        return remote(xbuf.at[c, half], xbuf.at[c, half], par_s.at[c], par_r.at[c], partner)
-
-    def first_ring(unit, dst):
-        return remote(xbuf.at[0, pl.ds(unit * UNIT, UNIT)], xbuf.at[dst, half],
-                      ring_s.at[dst], ring_r.at[dst], nxt)
-
-    own_copy.wait_recv()
-    first_ring(0, 1).start()
 
     loads[6].wait()
     lane = lax.broadcasted_iota(jnp.int32, (TOK, QW), 1)
@@ -209,13 +214,17 @@
     l_ref[...] = jnp.zeros(l_ref.shape, f32)
     acc[...] = jnp.zeros(acc.shape, f32)
 
-    far_copy.wait_recv()
-    far_share.start()
     n2_copy.wait_recv()
     for group in (0, 1):
         queries(group, n2buf[0])
-    far_share.wait_recv()
-    first_ring(1, 2).start()
+    for way in range(2):
+        ring(way, 1, 1).wait_recv()
+        ring(way, 1, 3).start()
+        share(way, 1).start()
+    far_copy.wait_recv()
+    far_share.start()
+    for way in range(2):
+        hop(far, way, 2).start()
     loads[7].wait()
     loads[8].wait()
 
@@ -229,10 +238,10 @@
             k_all[rows, cut] = matmul(xc, wkv[:, cut]).astype(bf16)
             v_all[rows, cut] = matmul(xc, wvv[:, cut]).astype(bf16)
 
-    ring(0, 1).wait_recv()
-    ring(1, 3).start()
-    share(1).start()
-    share(1).wait_recv()
+    own_copy.wait_recv()
+    for way in range(2):
+        share(way, 1).wait_recv()
+    far_share.wait_recv()
     project(0)
 
     half_lane = lax.broadcasted_iota(jnp.int32, (TOK, 128), 1) < HD
@@ -289,22 +298,26 @@
         shift = mask(p)
         scores(p, 1)
         attend(p, 0, shift)
-        ring(even, even).wait_recv()
-        share(even).start()
-        ring(even + last * (core - 1), even + 2 - last).start()
+        for way in range(2):
+            ring(way, even, even).wait_recv()
+            ring(way, even - last * (1 - way), even + 2 - last).start()
+            share(way, even).start()
         scores(p, 2)
         attend(p, 1, shift)
-        ring(odd, odd).wait_recv()
-        share(odd).start()
+        for way in range(2):
+            ring(way, odd, odd).wait_recv()
+            share(way, odd).start()
 
         @pl.when(p == 0)
         def _():
-            ring(odd, odd + 2).start()
+            for way in range(2):
+                ring(way, odd, odd + 2).start()
 
         scores(p, 3)
         attend(p, 2, shift)
-        share(even).wait_recv()
-        share(odd).wait_recv()
+        for way in range(2):
+            share(way, even).wait_recv()
+            share(way, odd).wait_recv()
         project(p + 1)
         scores(p + 1, 0)
         attend(p, 3, shift)
@@ -341,8 +354,9 @@
     for copy in halos + [own_copy, far_copy, far_share, n2_copy, att_copy]:
         copy.wait_send()
     for c in range(1, NCHUNK):
-        ring(c, c).wait_send()
-        share(c).wait_send()
+        for way in range(2):
+            ring(way, c, c).wait_send()
+            share(way, c).wait_send()
 
 
 def local(tokens, tissue, dw_kernel, w_fc1, w_fc2, layer_scale, w_query, w_key, w_value, w_out):
@@ -366,7 +380,7 @@
             vmem((GROUPS, 4 * TOK, 128), f32), vmem((GROUPS, 4 * TOK, 128), f32),
             vmem((2, 4 * TOK, 128), f32), vmem((2, TOK, HALF), f32),
             vmem((TOK, HALF), bf16), vmem((TOK, HALF), bf16),
-            sem((11,)), sem((9,)), sem((9,)), sem((NCHUNK,)), sem((NCHUNK,)), sem((NCHUNK,)), sem((NCHUNK,)),
+            sem((11,)), sem((9,)), sem((9,)), sem((2 * NCHUNK,)), sem((2 * NCHUNK,)), sem((2 * NCHUNK,)), sem((2 * NCHUNK,)),
         ],
         compiler_params=pltpu.CompilerParams(
             collective_id=0, has_side_effects=True, vmem_limit_bytes=60 << 20),

time: 55.9 us -> 55.2 us (0.987)
  Pallas kernels: 54.2 us -> 53.5 us
    pallas_call x1, Pallas kernels: 54.2 us -> 53.5 us  [local(): pl.pallas_call(kernel, out_shape=jax.ShapeDtypeStruct((ROWS, GW, C), bf16...]
where the time goes in v4:
time: 55.2 us; the launch traced here: 55.1 us
  Pallas kernels  53.5 us (97%)
  local copies, waits for them, and re-layouts  1.59 us (3%)
    pallas_call x1, Pallas kernels, local(): pl.pallas_call(kernel, out_shape=jax.ShapeDtypeStruct((ROWS, GW, C), bf16...  53.5 us
    unnamed x1, local copies, waits for them, and re-layouts  1.59 us

profile of v4, /device:TPU:1, one launch (start us, length us, event | category | flops | bytes accessed | tf_op | source)
XLA Modules:
  0.0 55.1 jit_solution(641296954561185255)
XLA Ops:
  0.0 53.5 %block.1 = bf16[3,64,384]{2,1,0:T(8,128)(2,1)} custom-call(bf16[3,64,384]{2,1,0:T(8,128)(2,1)} %tokens.1, s32[3,64]{1,0:T(4,128)} %tissue.1, bf16[7,7,384]{2,1,0:T(8,128)(2,1)} %dw.1, bf16[384,1536]{1,0:T(8,128)(2,1)} %w1.1, bf16[1536,384]{1,0:T(8,128)(2,1)} %w2.1, f32[384]{0:T(512)} %scale.1, bf16[384,1024]{1,0:T(8,128)(2,1)} %wq.1, bf16[384,1024]{1,0:T(8,128)(2,1)} %wk.1, ...), custom_call_target="tpu_custom_call" | custom-call | tf_op jit(solution)/shard_map/block/pallas_call | solution.py:364
  53.5 1.6 %copy.12 = bf16[3,64,384]{2,1,0:T(8,128)(2,1)} copy(bf16[3,64,384]{2,1,0:T(8,128)(2,1)} %block.1) | data formatting | bytes 294912

commit v5 on v4

--- a/solution.py
+++ b/solution.py
@@ -246,16 +246,36 @@
 
     half_lane = lax.broadcasted_iota(jnp.int32, (TOK, 128), 1) < HD
 
+    def score_part(p, g, n):
+        rows = pl.ds(pl.multiple_of(p * KS + n * 256, 256), 256)
+        s_ref[g % 2, :, n * 256 : (n + 1) * 256] = lax.dot_general(
+            qblk[g], k_all[rows, (g % 2) * QW : (g % 2 + 1) * QW], LAST, preferred_element_type=f32)
+
     def scores(p, g):
+        for n in range(3):
+            score_part(p, g, n)
+
+    def weigh(p, g):
+        at = g % 2
         rows = pl.ds(pl.multiple_of(p * KS, KS), KS)
-        s_ref[g % 2] = lax.dot_general(
-            qblk[g], k_all[rows, (g % 2) * QW : (g % 2 + 1) * QW], LAST, preferred_element_type=f32)
-
-    def attend(p, g, shift):
+        o = matmul(p_ref[at], v_all[rows, (g % 2) * QW : (g % 2 + 1) * QW])
+        for t in range(2):
+            a, b = slice(2 * t * TOK, (2 * t + 1) * TOK), slice((2 * t + 1) * TOK, (2 * t + 2) * TOK)
+            cut = slice(t * 128, (t + 1) * 128)
+            o_t = jnp.where(half_lane, o[a, cut], o[b, cut])
+            f_t = jnp.where(half_lane, a_ref[at, a, :], a_ref[at, b, :])
+            dst = slice((g % 2) * QW + t * 128, (g % 2) * QW + (t + 1) * 128)
+            acc[g // 2, :, dst] = acc[g // 2, :, dst] * f_t + o_t
+
+    def attend(p, g, shift, ahead=None, behind=None):
         at = g % 2
         tiles = range(KS // 128)
         for r in range(0, 4 * TOK, 32):
             rs = slice(r, r + 32)
+            if ahead is not None and r % 256 == 0:
+                score_part(*ahead, r // 256)
+            if behind is not None and r == 128:
+                weigh(*behind)
             st = [
                 (s_ref[at, rs, t * 128 : (t + 1) * 128].reshape(4, 8, 128)
                  + shift[:, t * 128 : (t + 1) * 128][None]).reshape(32, 128)
@@ -273,16 +293,6 @@
                 p_ref[at, rs, t * 128 : (t + 1) * 128] = weight.astype(bf16)
                 total = weight if total is None else total + weight
             l_ref[g, rs, :] = l_ref[g, rs, :] * factor + total
-        rows = pl.ds(pl.multiple_of(p * KS, KS), KS)
-        o = matmul(p_ref[at], v_all[rows, (g % 2) * QW : (g % 2 + 1) * QW])
-        for t in range(2):
-            a, b = slice(2 * t * TOK, (2 * t + 1) * TOK), slice((2 * t + 1) * TOK, (2 * t + 2) * TOK)
-            cut = slice(t * 128, (t + 1) * 128)
-            o_t = jnp.where(half_lane, o[a, cut], o[b, cut])
-            f_t = jnp.where(half_lane, a_ref[at, a, :], a_ref[at, b, :])
-            dst = slice((g % 2) * QW + t * 128, (g % 2) * QW + (t + 1) * 128)
-            acc[g // 2, :, dst] = acc[g // 2, :, dst] * f_t + o_t
-
     def mask(p):
         marks = [
             lax.dot_general(first_lane, xbuf[2 * p + i], LAST, preferred_element_type=f32) for i in range(2)
@@ -294,33 +304,49 @@
     @pl.loop(0, 3)
     def _(p):
         even, odd = 2 * p + 2, 2 * p + 3
-        last = lax.div(p, 2)
         shift = mask(p)
-        scores(p, 1)
-        attend(p, 0, shift)
-        for way in range(2):
-            ring(way, even, even).wait_recv()
-            ring(way, even - last * (1 - way), even + 2 - last).start()
-            share(way, even).start()
-        scores(p, 2)
-        attend(p, 1, shift)
+
+        def take_even():
+            for way in range(2):
+                ring(way, even, even).wait_recv()
+
+            @pl.when(p < 2)
+            def _():
+                for way in range(2):
+                    ring(way, even, even + 2).start()
+
+            @pl.when(p == 2)
+            def _():
+                ring(1, even, 7).start()
+
+            for way in range(2):
+                share(way, even).start()
+
+        pl.when(p > 0)(take_even)
+        attend(p, 0, shift, (p, 1))
+        pl.when(p == 0)(take_even)
+        attend(p, 1, shift, (p, 2), (p, 0))
         for way in range(2):
             ring(way, odd, odd).wait_recv()
-            share(way, odd).start()
+
+        @pl.when(p < 2)
+        def _():
+            ring(0, odd, odd + 2).start()
 
         @pl.when(p == 0)
         def _():
-            for way in range(2):
-                ring(way, odd, odd + 2).start()
-
-        scores(p, 3)
-        attend(p, 2, shift)
+            ring(1, odd, odd + 2).start()
+
+        for way in range(2):
+            share(way, odd).start()
+
+        attend(p, 2, shift, (p, 3), (p, 1))
         for way in range(2):
             share(way, even).wait_recv()
             share(way, odd).wait_recv()
         project(p + 1)
-        scores(p + 1, 0)
-        attend(p, 3, shift)
+        attend(p, 3, shift, (p + 1, 0), (p, 2))
+        weigh(p, 3)
 
     def attended(who):
         parts = []
@@ -334,15 +360,14 @@
         return jnp.concatenate(parts, axis=1)
 
     shift = mask(3)
-    scores(3, 1)
-    attend(3, 0, shift)
-    scores(3, 2)
-    attend(3, 1, shift)
+    attend(3, 0, shift, (3, 1))
+    attend(3, 1, shift, (3, 2), (3, 0))
+    weigh(3, 1)
     att_out[...] = attended(0)
     att_copy.start()
-    scores(3, 3)
-    attend(3, 2, shift)
-    attend(3, 3, shift)
+    attend(3, 2, shift, (3, 3))
+    attend(3, 3, shift, None, (3, 2))
+    weigh(3, 3)
 
     loads[9].wait()
     loads[10].wait()

time: 55.2 us -> 52.7 us (0.955)
  Pallas kernels: 53.5 us -> 51 us
    pallas_call x1, Pallas kernels: 53.5 us -> 51 us  [local(): pl.pallas_call(kernel, out_shape=jax.ShapeDtypeStruct((ROWS, GW, C), bf16...]
where the time goes in v5:
time: 52.7 us; the launch traced here: 52.6 us
  Pallas kernels  51 us (97%)
  local copies, waits for them, and re-layouts  1.59 us (3%)
    pallas_call x1, Pallas kernels, local(): pl.pallas_call(kernel, out_shape=jax.ShapeDtypeStruct((ROWS, GW, C), bf16...  51 us
    unnamed x1, local copies, waits for them, and re-layouts  1.59 us

profile of v5, /device:TPU:1, one launch (start us, length us, event | category | flops | bytes accessed | tf_op | source)
XLA Modules:
  0.0 52.6 jit_solution(424997544217172739)
XLA Ops:
  0.0 51.0 %block.1 = bf16[3,64,384]{2,1,0:T(8,128)(2,1)} custom-call(bf16[3,64,384]{2,1,0:T(8,128)(2,1)} %tokens.1, s32[3,64]{1,0:T(4,128)} %tissue.1, bf16[7,7,384]{2,1,0:T(8,128)(2,1)} %dw.1, bf16[384,1536]{1,0:T(8,128)(2,1)} %w1.1, bf16[1536,384]{1,0:T(8,128)(2,1)} %w2.1, f32[384]{0:T(512)} %scale.1, bf16[384,1024]{1,0:T(8,128)(2,1)} %wq.1, bf16[384,1024]{1,0:T(8,128)(2,1)} %wk.1, ...), custom_call_target="tpu_custom_call" | custom-call | tf_op jit(solution)/shard_map/block/pallas_call | solution.py:389
  51.0 1.6 %copy.12 = bf16[3,64,384]{2,1,0:T(8,128)(2,1)} copy(bf16[3,64,384]{2,1,0:T(8,128)(2,1)} %block.1) | data formatting | bytes 294912

commit v6 on v5

--- a/solution.py
+++ b/solution.py
@@ -306,25 +306,24 @@
         even, odd = 2 * p + 2, 2 * p + 3
         shift = mask(p)
 
-        def take_even():
+        def take(c):
             for way in range(2):
-                ring(way, even, even).wait_recv()
-
-            @pl.when(p < 2)
+                ring(way, c, c).wait_recv()
+
+            @pl.when(c < 6)
             def _():
-                for way in range(2):
-                    ring(way, even, even + 2).start()
-
-            @pl.when(p == 2)
-            def _():
-                ring(1, even, 7).start()
-
+                ring(0, c, c + 2).start()
+
+            ring(1, c, lax.min(c + 2, 7)).start()
             for way in range(2):
-                share(way, even).start()
-
-        pl.when(p > 0)(take_even)
+                share(way, c).start()
+
         attend(p, 0, shift, (p, 1))
-        pl.when(p == 0)(take_even)
+
+        @pl.when(p == 0)
+        def _():
+            take(even)
+
         attend(p, 1, shift, (p, 2), (p, 0))
         for way in range(2):
             ring(way, odd, odd).wait_recv()
@@ -345,6 +344,11 @@
             share(way, even).wait_recv()
             share(way, odd).wait_recv()
         project(p + 1)
+
+        @pl.when(p < 2)
+        def _():
+            take(even + 2)
+
         attend(p, 3, shift, (p + 1, 0), (p, 2))
         weigh(p, 3)
 

time: 52.7 us -> 53.6 us (1.017)
  Pallas kernels: 51 us -> 51.9 us
    pallas_call x1, Pallas kernels: 51 us -> 51.9 us  [local(): pl.pallas_call(kernel, out_shape=jax.ShapeDtypeStruct((ROWS, GW, C), bf16...]
where the time goes in v6:
time: 53.6 us; the launch traced here: 53.5 us
  Pallas kernels  51.9 us (97%)
  local copies, waits for them, and re-layouts  1.59 us (3%)
    pallas_call x1, Pallas kernels, local(): pl.pallas_call(kernel, out_shape=jax.ShapeDtypeStruct((ROWS, GW, C), bf16...  51.9 us
    unnamed x1, local copies, waits for them, and re-layouts  1.59 us

profile of v6, /device:TPU:1, one launch (start us, length us, event | category | flops | bytes accessed | tf_op | source)
XLA Modules:
  0.0 53.5 jit_solution(7635683944828714697)
XLA Ops:
  0.0 51.9 %block.1 = bf16[3,64,384]{2,1,0:T(8,128)(2,1)} custom-call(bf16[3,64,384]{2,1,0:T(8,128)(2,1)} %tokens.1, s32[3,64]{1,0:T(4,128)} %tissue.1, bf16[7,7,384]{2,1,0:T(8,128)(2,1)} %dw.1, bf16[384,1536]{1,0:T(8,128)(2,1)} %w1.1, bf16[1536,384]{1,0:T(8,128)(2,1)} %w2.1, f32[384]{0:T(512)} %scale.1, bf16[384,1024]{1,0:T(8,128)(2,1)} %wq.1, bf16[384,1024]{1,0:T(8,128)(2,1)} %wk.1, ...), custom_call_target="tpu_custom_call" | custom-call | tf_op jit(solution)/shard_map/block/pallas_call | solution.py:393
  51.9 1.6 %copy.12 = bf16[3,64,384]{2,1,0:T(8,128)(2,1)} copy(bf16[3,64,384]{2,1,0:T(8,128)(2,1)} %block.1) | data formatting | bytes 294912
